TPU v7x, 32 devices: a whole 2x2x4 slice. The times are simulated.
32 devices in a mesh: parts: 2 (over x), row: 16 (over z, y, core).
Axes of the slice: x: 2, y: 2, z: 4, core: 2. Of those that a mesh axis runs over, the one named last changes fastest.
Arguments:
- coords: int32 [4, 3, 512], P('parts'), parts along dimension 0, may hold values from 0 to 7
- labels: int32 [16, 16, 512], P('parts', 'row'), parts along dimension 0, may hold values from 0 to 255
- ranks: int32 [16, 16, 2], P('parts', 'row'), parts along dimension 0, may hold values from 16 to 128, as said below
- u_first: bfloat16 [16, 16, 512, 128], P('parts', 'row'), parts along dimension 0, may hold values from -6 to 6
- v_first: bfloat16 [16, 16, 512, 128], P('parts', 'row'), parts along dimension 0, may hold values from -0.0046875 to 0.0046875
- u_second: bfloat16 [16, 16, 512, 128], P('parts', 'row'), parts along dimension 0, may hold values from -6 to 6
- v_second: bfloat16 [16, 16, 512, 128], P('parts', 'row'), parts along dimension 0, may hold values from -0.01171875 to 0.01171875
Outputs:
- eliminated: float32 [16, 16, 512, 256], P('parts', 'row'), parts along dimension 0
- diagonal_factors: float32 [4, 512, 512], P('parts'), parts along dimension 0
There are 2 independent parts, one for each index of `parts`. A program takes and returns all parts, laid end to end along the dimension named above; each array names one. Nothing has to cross between parts.
Inputs may be any that keep to these rules, and one draw needn't show every extreme that they name: `ranks`: the block of tile 1 in column 0 has rank 128; some block has rank 128 // 8.
All inputs are finite; a program needn't handle non-finite values.
Results may differ from a plain program's by a relative error of at most 0.0003.
Values may be sent and summed in bfloat16 or wider, within the bound.
No kernel may reach another device: no remote copies, remote signals or barrier semaphores. Data moves between devices by JAX's collectives and lax.ppermute only.
A program may use at most 128 MiB of HBM per device.

v0:
```python
import math
import jax
import jax.numpy as jnp
from jax import lax
from jax.sharding import PartitionSpec as P

NRHS = 256
highest = lax.Precision.HIGHEST
four_pi = 4.0 * math.pi


def spread(shard, axis, root):
    mine = lax.axis_index(axis) == root
    return lax.psum(jnp.where(mine, shard, jnp.zeros_like(shard)), axis)


def matmul(left, right):
    return jnp.dot(left, right, precision=highest, preferred_element_type=jnp.float32)


def kernel_tile(points):
    spots = points.astype(jnp.float32)
    distance = jnp.zeros((spots.shape[1], spots.shape[1]), jnp.float32)
    for dimension in range(3):
        offset = spots[dimension][:, None] - spots[dimension][None, :]
        distance = distance + offset * offset
    return 1.0 / (four_pi * jnp.sqrt(distance + 1.0)) + jnp.eye(spots.shape[1], dtype=jnp.float32)


def onehot(label_row):
    return (label_row[..., None] == jnp.arange(NRHS, dtype=jnp.int32)).astype(jnp.float32)


def triangular(lower, target):
    return lax.linalg.triangular_solve(lower, target, left_side=True, lower=True)


def solve_stack(lower, stack):
    number, height, breadth = stack.shape
    flat = jnp.transpose(stack, (1, 0, 2)).reshape(height, number * breadth)
    solved = triangular(lower, flat)
    return jnp.transpose(solved.reshape(height, number, breadth), (1, 0, 2))


def rank_mask(rank_values, breadth):
    columns = jnp.arange(breadth, dtype=jnp.int32)
    return (columns[None, :] < rank_values[:, None]).astype(jnp.float32)


def second_panel(points, label_row, u_one, w_one, first_sol):
    inner_gram = matmul(w_one.T, w_one)
    diagonal_tile = kernel_tile(points) - matmul(matmul(u_one, inner_gram), u_one.T)
    lower = jnp.linalg.cholesky(diagonal_tile)
    target = onehot(label_row) - matmul(u_one, matmul(w_one.T, first_sol))
    return (lower, triangular(lower, target))


def update(
    w_tiles, first_sol, second_lower, second_sol, u_one, w_one, label_rows, rank_rows, u0, u1, v1
):
    breadth = u0.shape[-1]
    u_zero = u0.astype(jnp.float32)
    u_next = u1.astype(jnp.float32)
    v_next = v1.astype(jnp.float32) * rank_mask(rank_rows[:, 1], breadth)[:, None, :]
    first_weights = jnp.einsum("nbr,bc->nrc", w_tiles, first_sol, precision=highest)
    first_update = jnp.einsum("nbr,nrc->nbc", u_zero, first_weights, precision=highest)
    cross = jnp.einsum("br,nbs->nrs", w_one, w_tiles, precision=highest)
    mixed = -jnp.einsum("br,nrs->nbs", u_one, cross, precision=highest)
    factor = solve_stack(second_lower, jnp.concatenate([v_next, mixed], axis=-1))
    second_weights = jnp.einsum("nbk,bc->nkc", factor, second_sol, precision=highest)
    left_pair = jnp.concatenate([u_next, u_zero], axis=-1)
    second_update = jnp.einsum("nbk,nkc->nbc", left_pair, second_weights, precision=highest)
    return onehot(label_rows) - first_update - second_update


def local(coords, labels, ranks, u_first, v_first, u_second, v_second):
    position = lax.axis_index("row")
    label_rows = labels[:, 0]
    rank_rows = ranks[:, 0]
    u_zero = u_first[:, 0]
    v_zero = v_first[:, 0]
    height = u_zero.shape[1]
    breadth = u_zero.shape[2]
    w_tiles = None

    def first_factor():
        lower = jnp.linalg.cholesky(kernel_tile(coords[0]))
        return (lower, triangular(lower, onehot(label_rows[0])))

    def first_empty():
        return (jnp.zeros((height, height), jnp.float32), jnp.zeros((height, NRHS), jnp.float32))

    first_lower, first_sol = lax.cond(position == 0, first_factor, first_empty)
    first_lower, first_sol = (spread(first_lower, "row", 0), spread(first_sol, "row", 0))
    masked = v_zero.astype(jnp.float32) * rank_mask(rank_rows[:, 0], breadth)[:, None, :]
    w_tiles = solve_stack(first_lower, masked)

    def second_factor():
        u_pick = u_zero[0].astype(jnp.float32)
        w_pick = w_tiles[0]
        lower, solved = second_panel(coords[1], label_rows[0], u_pick, w_pick, first_sol)
        return (lower, solved, u_pick, w_pick)

    def second_empty():
        return (
            jnp.zeros((height, height), jnp.float32),
            jnp.zeros((height, NRHS), jnp.float32),
            jnp.zeros((height, breadth), jnp.float32),
            jnp.zeros((height, breadth), jnp.float32),
        )

    second_lower, second_sol, u_one, w_one = lax.cond(position == 1, second_factor, second_empty)
    second_lower, second_sol, u_one, w_one = (
        spread(second_lower, "row", 1),
        spread(second_sol, "row", 1),
        spread(u_one, "row", 1),
        spread(w_one, "row", 1),
    )
    updated = update(
        w_tiles,
        first_sol,
        second_lower,
        second_sol,
        u_one,
        w_one,
        label_rows,
        rank_rows,
        u_zero,
        u_second[:, 0],
        v_second[:, 0],
    )
    leading = jnp.where(position == 0, first_sol, jnp.where(position == 1, second_sol, updated[0]))
    updated = updated.at[0].set(leading)
    return (updated[:, None], jnp.stack([first_lower, second_lower]))


def solution(mesh):
    in_specs = (
        P("parts", None, None),
        P("parts", "row", None),
        P("parts", "row", None),
        P("parts", "row", None, None),
        P("parts", "row", None, None),
        P("parts", "row", None, None),
        P("parts", "row", None, None),
    )
    out_specs = (P("parts", "row", None, None), P("parts", None, None))
    return jax.shard_map(local, mesh=mesh, in_specs=in_specs, out_specs=out_specs, check_vma=False)
```

profile of v0, /device:TPU:0, one launch (start us, length us, event | category | flops | bytes accessed | tf_op | source)
XLA Modules:
  0.0 670.5 jit_solution(9478993667882919614)
XLA Ops:
  7.9 145.0 %conditional.2 = (f32[512,512]{1,0:T(8,128)S(1)}, f32[512,256]{0,1:T(8,128)}) conditional(s32[]{:T(128)} %convert_element_type.64, () %tuple.30, (s32[2,3,512]{2,0,1:T(2,128)}, s32[8,512]{1,0:T(8,128)S(1)}) %tuple.157), branch_computations={%region_0.0_spmd, %region_1.12_spmd} | conditional | flops 916293632 | bytes 19471616 | solution.py:93
  11.5 11.7 %cholesky.286 = f32[128,128]{1,0:T(8,128)S(1)} custom-call(f32[128,128]{1,0:T(8,128)S(1)} %cholesky.426), custom_call_target="Cholesky" | custom-call | tf_op jit(solution)/shard_map/cond/branch_1_fun/jit(cholesky)/cholesky | solution.py:87
  23.3 9.8 %custom-call.35 = f32[1,128,128]{1,2,0:T(8,128)S(1)} custom-call(f32[1,128,128]{2,1,0:T(8,128)S(1)} %get-tuple-element.160), custom_call_target="InvertDiagBlocksLowerTriangular" | custom-call | tf_op jit(solution)/shard_map/cond/branch_1_fun/jit(cholesky)/cholesky | solution.py:87
  33.9 12.0 %cholesky.305 = f32[128,128]{1,0:T(8,128)S(1)} custom-call(f32[128,128]{1,0:T(8,128)S(1)} %cholesky.430), custom_call_target="Cholesky" | custom-call | tf_op jit(solution)/shard_map/cond/branch_1_fun/jit(cholesky)/cholesky | solution.py:87
  47.9 9.8 %custom-call.36 = f32[1,128,128]{1,2,0:T(8,128)S(1)} custom-call(f32[1,128,128]{2,1,0:T(8,128)S(1)} %get-tuple-element.157), custom_call_target="InvertDiagBlocksLowerTriangular" | custom-call | tf_op jit(solution)/shard_map/cond/branch_1_fun/jit(cholesky)/cholesky | solution.py:87
  58.4 11.7 %cholesky.326 = f32[128,128]{1,0:T(8,128)S(1)} custom-call(f32[128,128]{1,0:T(8,128)S(1)} %cholesky.435), custom_call_target="Cholesky" | custom-call | tf_op jit(solution)/shard_map/cond/branch_1_fun/jit(cholesky)/cholesky | solution.py:87
  71.5 9.8 %custom-call.37 = f32[1,128,128]{1,2,0:T(8,128)S(1)} custom-call(f32[1,128,128]{2,1,0:T(8,128)S(1)} %get-tuple-element.154), custom_call_target="InvertDiagBlocksLowerTriangular" | custom-call | tf_op jit(solution)/shard_map/cond/branch_1_fun/jit(cholesky)/cholesky | solution.py:87
  81.9 11.7 %cholesky.343 = f32[128,128]{1,0:T(8,128)S(1)} custom-call(f32[128,128]{1,0:T(8,128)S(1)} %convolution_subtract_fusion.5), custom_call_target="Cholesky" | custom-call | tf_op jit(solution)/shard_map/cond/branch_1_fun/jit(cholesky)/cholesky | solution.py:87
  95.3 10.6 %while.7 = (s32[]{:T(128)}, f32[512,512]{1,0:T(8,128)S(1)}, s32[4,2]{0,1:T(2,128)S(1)}, f32[4,128,128]{2,1,0:T(8,128)}, s32[]{:T(128)}) while((s32[]{:T(128)}, f32[512,512]{1,0:T(8,128)S(1)}, s32[4,2]{0,1:T(2,128)S(1)}, f32[4,128,128]{2,1,0:T(8,128)}, s32[]{:T(128)}) %tuple.135), condition=%wide.while_cond.1, body=%wide.while_body.1.sunk | while | flops 2 | bytes 132205 | solution.py:35
  105.8 40.1 %custom-call.38 = f32[4,128,128]{1,2,0:T(8,128)S(1)} custom-call(f32[4,128,128]{2,1,0:T(8,128)} %get-tuple-element.79), custom_call_target="InvertDiagBlocksLowerTriangular" | custom-call | tf_op jit(solution)/shard_map/cond/branch_1_fun/triangular_solve/custom-call.3 | solution.py:35
  158.0 92.5 %all-reduce.8.cloned.1.call-done = (f32[512,256]{0,1:T(8,128)}, f32[512,512]{1,0:T(8,128)}) async-done(((f32[512,256]{0,1:T(8,128)}, f32[512,512]{1,0:T(8,128)}), (f32[512,256]{0,1:T(8,128)}, f32[512,512]{1,0:T(8,128)})) %all-reduce.8.cloned.1.call-update) | async-done | bytes 1572880 | tf_op jit(solution)/shard_map/psum | solution.py:14
  251.9 8.0 %while.9 = (s32[]{:T(128)}, f32[512,512]{1,0:T(8,128)S(1)}, s32[4,2]{0,1:T(2,128)S(1)}, f32[4,128,128]{2,1,0:T(8,128)S(1)}, s32[]{:T(128)}) while((s32[]{:T(128)}, f32[512,512]{1,0:T(8,128)S(1)}, s32[4,2]{0,1:T(2,128)S(1)}, f32[4,128,128]{2,1,0:T(8,128)S(1)}, s32[]{:T(128)}) %tuple.140), condition=%wide.while_cond.2, body=%wide.while_body.2.sunk | while | flops 2 | bytes 131189 | solution.py:35
  259.9 39.3 %custom-call.29 = f32[4,128,128]{1,2,0:T(8,128)S(1)} custom-call(f32[4,128,128]{2,1,0:T(8,128)S(1)} %get-tuple-element.64), custom_call_target="InvertDiagBlocksLowerTriangular" | custom-call | tf_op jit(solution)/shard_map/triangular_solve | solution.py:35
  309.7 10.4 %conditional.3 = (f32[512,512]{1,0:T(8,128)}, f32[512,128]{1,0:T(8,128)}, f32[512,128]{1,0:T(8,128)S(1)}, f32[512,256]{0,1:T(8,128)}) conditional(s32[]{:T(128)} %convert_element_type.69, () %tuple.32, (s32[2,3,512]{2,0,1:T(2,128)S(1)}, f32[8,512,128]{2,1,0:T(8,128)}, bf16[8,512,128]{2,1,0:T(8,128)(2,1)S(1)}, s32[8,512]{1,0:T(8,128)S(1)}, ...), branch_computations={%region_12.15_spmd, %region_13.16_spmd} | conditional | flops 1919715328 | bytes 30088544 | solution.py:112
  328.0 3.8 fusion.134
  331.8 234.4 %all-reduce.6.cloned.1.call-done = (f32[512,128]{1,0:T(8,128)}, f32[512,128]{1,0:T(8,128)}, f32[512,512]{1,0:T(8,128)}, f32[512,256]{0,1:T(8,128)}) async-done(((f32[512,128]{1,0:T(8,128)}, f32[512,128]{1,0:T(8,128)}, f32[512,512]{1,0:T(8,128)}, f32[512,256]{0,1:T(8,128)}), (f32[512,128]{1,0:T(8,128)}, f32[512,128]{1,0:T(8,128)}, f32[512,512]{1,0:T(8,128)}, ...) | async-done | bytes 2097168 | tf_op jit(solution)/shard_map/psum | solution.py:14
  566.3 5.6 convolution_bitcast_fusion.1
  572.0 8.2 %while.10 = (s32[]{:T(128)}, f32[512,512]{1,0:T(8,128)S(1)}, s32[4,2]{0,1:T(2,128)S(1)}, f32[4,128,128]{2,1,0:T(8,128)S(1)}, s32[]{:T(128)}) while((s32[]{:T(128)}, f32[512,512]{1,0:T(8,128)S(1)}, s32[4,2]{0,1:T(2,128)S(1)}, f32[4,128,128]{2,1,0:T(8,128)S(1)}, s32[]{:T(128)}) %tuple.156), condition=%wide.while_cond.3, body=%wide.while_body.3.sunk | while | flops 2 | bytes 131189 | solution.py:35
  580.9 40.3 %custom-call.30 = f32[4,128,128]{1,2,0:T(8,128)S(1)} custom-call(f32[4,128,128]{2,1,0:T(8,128)} %copy-done.22), custom_call_target="InvertDiagBlocksLowerTriangular" | custom-call | tf_op jit(solution)/shard_map/triangular_solve | solution.py:35
  621.2 2.9 negate_bitcast_fusion
  629.1 3.5 convolution_subtract_fusion.13
  633.7 5.5 fusion.80
  642.9 7.8 %fusion.72 = f32[8,256,256]{2,1,0:T(8,128)S(1)} fusion(f32[8,512,256]{2,0,1:T(8,128)S(1)} %bitcast.272, f32[512,256]{0,1:T(8,128)S(1)} %copy-done.17), kind=kOutput, calls=%fused_computation.162 | convolution fusion | flops 3221225472 | bytes 6815744 | tf_op jit(solution)/shard_map/nbk,bc->nkc/dot_general | solution.py:70
  656.2 5.5 copy.35
  (168 shorter events, 86.8 us)
Async XLA Ops:
  7.2 243.3 %all-reduce.8.cloned.1.call-start = ((), (), s32[]{:S(2)}) async-start(), calls=%async_computation.1 | async-start | bytes 3145728 | tf_op jit(solution)/shard_map/psum | solution.py:14
  153.0 3.1 copy-start.24
  153.0 3.1 copy-start.20
  156.0 410.3 %all-reduce.6.cloned.1.call-start = ((), (), s32[]{:S(2)}) async-start(), calls=%async_computation | async-start | bytes 4194304 | tf_op jit(solution)/shard_map/psum | solution.py:14
  300.9 3.1 copy-start.18
  304.0 4.9 copy-start.6
  307.4 1.5 copy-start.15
  307.4 2.0 copy-start.3
  307.4 2.3 copy-start.12
  307.4 2.3 copy-start.23
  321.2 1.8 copy-start.21
  324.3 1.6 copy-start.7
  324.3 1.6 copy-start.13
  324.3 1.7 copy-start.16
  326.0 2.0 copy-start.4
  566.3 5.6 copy-start.9
  580.2 0.7 copy-start.22
  640.9 2.0 copy-start.17
  642.9 7.8 %copy-start = (f32[8,256,512]{2,1,0:T(8,128)S(1)}, f32[8,256,512]{2,1,0:T(8,128)}, u32[]{:S(2)}) copy-start(f32[8,256,512]{2,1,0:T(8,128)} %fusion.134) | copy-start | bytes 12582916
  642.9 7.8 %copy-start.5 = (bf16[8,1,512,128]{3,2,1,0:T(8,128)(2,1)S(1)}, bf16[8,1,512,128]{3,2,1,0:T(8,128)(2,1)}, u32[]{:S(2)}) copy-start(bf16[8,1,512,128]{3,2,1,0:T(8,128)(2,1)} %param.19) | copy-start | bytes 3145732
  642.9 7.8 %copy-start.19 = (bf16[8,1,512,128]{3,2,1,0:T(8,128)(2,1)S(1)}, bf16[8,1,512,128]{3,2,1,0:T(8,128)(2,1)}, u32[]{:S(2)}) copy-start(bf16[8,1,512,128]{3,2,1,0:T(8,128)(2,1)} %param.21) | copy-start | bytes 3145732
  653.3 2.0 copy-start.14
  656.2 5.5 copy-start.8
  656.2 5.5 copy-start.10
Sparse Core Ops, SparseCore 0:
  156.1 94.3 all-reduce.7
  323.0 243.1 all-reduce.5
where the time goes:
time: 680 us; the launch traced here: 670 us
  waiting for transfers between devices  327 us (48%)
  other arithmetic  215 us (32%)
  matrix products  55.6 us (8%)
  local copies, waits for them, and re-layouts  46.8 us (7%)
  between operations  15 us (2%)
  loops' own time  10.8 us (2%)
    psum x2, waiting for transfers between devices, spread(): return lax.psum(jnp.where(mine, shard, jnp.zeros_like(shard)), axis)  327 us
    another operation x11, other arithmetic, triangular(): lax.linalg.triangular_solve(lower, target, left_side=True, lower=True)  122 us
    another operation x14, other arithmetic, first_factor(): lower = jnp.linalg.cholesky(kernel_tile(coords[0]))  78.8 us
    another operation x21, matrix products, triangular(): lax.linalg.triangular_solve(lower, target, left_side=True, lower=True)  29 us
    another operation x29, local copies, waits for them, and re-layouts  19.5 us
    unnamed x52, local copies, waits for them, and re-layouts  13.7 us
  transfers between devices with their start and end apart: 2, of which 2 were waited for; matrix products, arithmetic and copies ran while one was open for 2% of the time, Pallas kernels for 0%

commit v1 on v0

--- a/solution.py
+++ b/solution.py
@@ -11,7 +11,7 @@
 
 def spread(shard, axis, root):
     mine = lax.axis_index(axis) == root
-    return lax.psum(jnp.where(mine, shard, jnp.zeros_like(shard)), axis)
+    return jnp.sum(lax.all_gather(jnp.where(mine, shard, jnp.zeros_like(shard)), axis), axis=0)
 
 
 def matmul(left, right):

time: 680 us -> 1020 us (1.50)
  waiting for transfers between devices: 327 us -> 624 us
  other arithmetic: 215 us -> 250 us
  local copies, waits for them, and re-layouts: 46.8 us -> 66.2 us
  matrix products: 55.6 us -> 44.8 us
    all_gather x0 -> x6, waiting for transfers between devices: none -> 624 us  [spread(): lax.all_gather(jnp.where(mine, shard, jnp.zeros_like(shard)), axis)]
    psum x2 -> x0, waiting for transfers between devices: 327 us -> none  [spread(): return lax.psum(jnp.where(mine, shard, jnp.zeros_like(shard)), axis)]
    reduce_sum x0 -> x6, other arithmetic: none -> 30.3 us  [spread(): jnp.sum(lax.all_gather(jnp.where(mine, shard, jnp.zeros_like(shard)), axi...]
    another operation x11 -> x12, other arithmetic: 122 us -> 127 us  [triangular(): lax.linalg.triangular_solve(lower, target, left_side=True, lower=True)]
  transfers between devices with their start and end apart: 2 -> 6, of which waited for: 2 -> 6; matrix products, arithmetic and copies ran while one was open for 2% -> 5% of each run, Pallas kernels for 0% -> 0%
where the time goes in v1:
time: 1020 us; the launch traced here: 1010 us
  waiting for transfers between devices  624 us (61%)
  other arithmetic  250 us (25%)
  local copies, waits for them, and re-layouts  66.2 us (6%)
  matrix products  44.8 us (4%)
  between operations  15 us (1%)
  loops' own time  12.1 us (1%)
    all_gather x6, waiting for transfers between devices, spread(): lax.all_gather(jnp.where(mine, shard, jnp.zeros_like(shard)), axis)  624 us
    another operation x12, other arithmetic, triangular(): lax.linalg.triangular_solve(lower, target, left_side=True, lower=True)  127 us
    another operation x14, other arithmetic, first_factor(): lower = jnp.linalg.cholesky(kernel_tile(coords[0]))  78.7 us
    reduce_sum x6, other arithmetic, spread(): jnp.sum(lax.all_gather(jnp.where(mine, shard, jnp.zeros_like(shard)), axi...  30.3 us
    another operation x21, matrix products, triangular(): lax.linalg.triangular_solve(lower, target, left_side=True, lower=True)  24.3 us
    another operation x29, local copies, waits for them, and re-layouts  23.2 us
  transfers between devices with their start and end apart: 6, of which 6 were waited for; matrix products, arithmetic and copies ran while one was open for 5% of the time, Pallas kernels for 0%

profile of v1, /device:TPU:0, one launch (start us, length us, event | category | flops | bytes accessed | tf_op | source)
XLA Modules:
  0.0 1012.7 jit_solution(2576956888503549295)
XLA Ops:
  7.9 144.6 %conditional.2 = (f32[512,512]{1,0:T(8,128)S(1)}, f32[512,256]{1,0:T(8,128)}) conditional(s32[]{:T(128)} %convert_element_type.64, () %tuple.30, (s32[2,3,512]{2,0,1:T(2,128)}, s32[8,512]{1,0:T(8,128)S(1)}) %tuple.161), branch_computations={%region_0.0_spmd, %region_1.12_spmd} | conditional | flops 916293632 | bytes 18423040 | solution.py:93
  11.5 11.7 %cholesky.286 = f32[128,128]{1,0:T(8,128)S(1)} custom-call(f32[128,128]{1,0:T(8,128)S(1)} %cholesky.426), custom_call_target="Cholesky" | custom-call | tf_op jit(solution)/shard_map/cond/branch_1_fun/jit(cholesky)/cholesky | solution.py:87
  23.3 9.8 custom-call.35
  33.9 12.0 %cholesky.305 = f32[128,128]{1,0:T(8,128)S(1)} custom-call(f32[128,128]{1,0:T(8,128)S(1)} %cholesky.430), custom_call_target="Cholesky" | custom-call | tf_op jit(solution)/shard_map/cond/branch_1_fun/jit(cholesky)/cholesky | solution.py:87
  47.9 9.8 custom-call.36
  58.4 11.7 %cholesky.326 = f32[128,128]{1,0:T(8,128)S(1)} custom-call(f32[128,128]{1,0:T(8,128)S(1)} %cholesky.435), custom_call_target="Cholesky" | custom-call | tf_op jit(solution)/shard_map/cond/branch_1_fun/jit(cholesky)/cholesky | solution.py:87
  71.4 9.8 custom-call.37
  81.8 11.7 %cholesky.343 = f32[128,128]{1,0:T(8,128)S(1)} custom-call(f32[128,128]{1,0:T(8,128)S(1)} %convolution_subtract_fusion.5), custom_call_target="Cholesky" | custom-call | tf_op jit(solution)/shard_map/cond/branch_1_fun/jit(cholesky)/cholesky | solution.py:87
  95.0 10.6 %while.7 = (s32[]{:T(128)}, f32[512,512]{1,0:T(8,128)S(1)}, s32[4,2]{0,1:T(2,128)S(1)}, f32[4,128,128]{2,1,0:T(8,128)}, s32[]{:T(128)}) while((s32[]{:T(128)}, f32[512,512]{1,0:T(8,128)S(1)}, s32[4,2]{0,1:T(2,128)S(1)}, f32[4,128,128]{2,1,0:T(8,128)}, s32[]{:T(128)}) %tuple.133), condition=%wide.while_cond.1, body=%wide.while_body.1.sunk | while | flops 2 | bytes 132205 | solution.py:35
  105.6 40.1 %custom-call.38 = f32[4,128,128]{1,2,0:T(8,128)S(1)} custom-call(f32[4,128,128]{2,1,0:T(8,128)} %get-tuple-element.79), custom_call_target="InvertDiagBlocksLowerTriangular" | custom-call | tf_op jit(solution)/shard_map/cond/branch_1_fun/triangular_solve/custom-call.3 | solution.py:35
  159.4 68.9 %all-gather.15.cloned.1.call-done = f32[8192,256]{1,0:T(8,128)} async-done(((f32[512,256]{1,0:T(8,128)}), f32[8192,256]{1,0:T(8,128)}) %all-gather.15.cloned.1.call-update) | async-done | bytes 8388624 | tf_op jit(solution)/shard_map/all_gather | solution.py:14
  233.1 123.1 %all-gather.13.cloned.1.call-done = f32[8192,512]{1,0:T(8,128)} async-done(((f32[512,512]{1,0:T(8,128)}), f32[8192,512]{1,0:T(8,128)}) %all-gather.13.cloned.1.call-update) | async-done | bytes 16777232 | tf_op jit(solution)/shard_map/all_gather | solution.py:14
  356.2 7.9 reduce_sum.58
  364.3 8.0 while.9
  373.0 40.1 %custom-call.29 = f32[4,128,128]{1,2,0:T(8,128)S(1)} custom-call(f32[4,128,128]{2,1,0:T(8,128)} %copy-done.17), custom_call_target="InvertDiagBlocksLowerTriangular" | custom-call | tf_op jit(solution)/shard_map/triangular_solve | solution.py:35
  422.7 11.8 %conditional.3 = (f32[512,512]{1,0:T(8,128)}, f32[512,256]{1,0:T(8,128)}, f32[512,128]{1,0:T(8,128)}, f32[512,128]{1,0:T(8,128)S(1)}) conditional(s32[]{:T(128)} %convert_element_type.69, () %tuple.32, (s32[2,3,512]{2,0,1:T(2,128)S(1)}, f32[8,512,128]{1,2,0:T(8,128)S(1)}, bf16[8,512,128]{2,1,0:T(8,128)(2,1)}, s32[8,512]{1,0:T(8,128)S(1)}, ...), branch_computations={%region_12.15_spmd, %region_13.16_spmd} | conditional | flops 1919715328 | bytes 33234272 | solution.py:112
  452.3 198.7 %all-gather.19.cloned.1.call-done = f32[8192,128]{1,0:T(8,128)} async-done(((f32[512,128]{1,0:T(8,128)}), f32[8192,128]{1,0:T(8,128)}) %all-gather.19.cloned.1.call-update) | async-done | bytes 4194320 | tf_op jit(solution)/shard_map/all_gather | solution.py:14
  653.4 48.7 %all-gather.21.cloned.1.call-done = f32[8192,128]{1,0:T(8,128)} async-done(((f32[512,128]{1,0:T(8,128)}), f32[8192,128]{1,0:T(8,128)}) %all-gather.21.cloned.1.call-update) | async-done | bytes 4194320 | tf_op jit(solution)/shard_map/all_gather | solution.py:14
  715.5 62.1 %all-gather.23.cloned.1.call-done = f32[8192,256]{1,0:T(8,128)} async-done(((f32[512,256]{1,0:T(8,128)}), f32[8192,256]{1,0:T(8,128)}) %all-gather.23.cloned.1.call-update) | async-done | bytes 8388624 | tf_op jit(solution)/shard_map/all_gather | solution.py:14
  782.5 122.2 %all-gather.17.cloned.1.call-done = f32[8192,512]{1,0:T(8,128)} async-done(((f32[512,512]{1,0:T(8,128)}), f32[8192,512]{1,0:T(8,128)}) %all-gather.17.cloned.1.call-update) | async-done | bytes 16777232 | tf_op jit(solution)/shard_map/all_gather | solution.py:14
  904.7 8.1 reduce_sum.60
  914.0 11.9 %while.10 = (s32[]{:T(128)}, f32[512,512]{1,0:T(8,128)}, s32[4,2]{0,1:T(2,128)S(1)}, f32[4,128,128]{2,1,0:T(8,128)S(1)}, s32[]{:T(128)}) while((s32[]{:T(128)}, f32[512,512]{1,0:T(8,128)}, s32[4,2]{0,1:T(2,128)S(1)}, f32[4,128,128]{2,1,0:T(8,128)S(1)}, s32[]{:T(128)}) %tuple.160), condition=%wide.while_cond.3, body=%wide.while_body.3.sunk | while | flops 2 | bytes 131189 | solution.py:35
  926.6 40.1 %custom-call.30 = f32[4,128,128]{1,2,0:T(8,128)S(1)} custom-call(f32[4,128,128]{2,1,0:T(8,128)} %copy-done.16), custom_call_target="InvertDiagBlocksLowerTriangular" | custom-call | tf_op jit(solution)/shard_map/triangular_solve | solution.py:35
  981.9 5.6 copy.64
  (185 shorter events, 143.3 us)
Async XLA Ops:
  7.2 221.1 %all-gather.15.cloned.1.call-start = ((), (), s32[]{:S(2)}) async-start(), calls=%async_computation.1 | async-start | bytes 8912896 | tf_op jit(solution)/shard_map/all_gather | solution.py:14
  154.5 1.6 copy-start.14
  154.5 201.7 %all-gather.13.cloned.1.call-start = ((), (), s32[]{:S(2)}) async-start(), calls=%async_computation | async-start | bytes 17825792 | tf_op jit(solution)/shard_map/all_gather | solution.py:14
  155.6 1.0 copy-start.19
  155.7 495.4 %all-gather.19.cloned.1.call-start = ((), (), s32[]{:S(2)}) async-start(), calls=%async_computation.3 | async-start | bytes 4456448 | tf_op jit(solution)/shard_map/all_gather | solution.py:14
  372.3 0.7 copy-start.17
  415.4 2.0 copy-start.12
  420.8 1.9 copy-start.18
  435.3 266.8 %all-gather.21.cloned.1.call-start = ((), (), s32[]{:S(2)}) async-start(), calls=%async_computation.4 | async-start | bytes 4456448 | tf_op jit(solution)/shard_map/all_gather | solution.py:14
  436.1 341.4 %all-gather.23.cloned.1.call-start = ((), (), s32[]{:S(2)}) async-start(), calls=%async_computation.5 | async-start | bytes 8912896 | tf_op jit(solution)/shard_map/all_gather | solution.py:14
  437.0 467.7 %all-gather.17.cloned.1.call-start = ((), (), s32[]{:S(2)}) async-start(), calls=%async_computation.2 | async-start | bytes 17825792 | tf_op jit(solution)/shard_map/all_gather | solution.py:14
  445.3 3.1 copy-start.4
  705.2 1.8 copy-start.15
  707.0 1.8 copy-start.1
  781.5 123.2 %copy-start.6 = (f32[512,256]{1,0:T(8,128)}, f32[512,256]{1,0:T(8,128)S(1)}, u32[]{:S(2)}) copy-start(f32[512,256]{1,0:T(8,128)S(1)} %reduce_sum.63) | copy-start | bytes 1572868
  925.9 0.7 copy-start.16
  969.0 3.0 copy-start.8
  974.2 1.2 copy-start.7
  987.5 5.5 copy-start
  987.5 5.5 copy-start.5
  987.5 5.5 copy-start.13
  995.6 2.0 copy-start.10
  995.6 2.0 copy-start.11
Sparse Core Ops, SparseCore 0:
  154.6 73.5 all-gather.14
  231.0 125.1 all-gather.12
  435.4 215.5 all-gather.18
  653.0 49.0 all-gather.20
  704.1 73.3 all-gather.22
  779.6 125.1 all-gather.16
